TPU v7x, 32 devices: a whole 2x2x4 slice. The times are simulated.
32 devices in a mesh: scene: 2 (over y), tok: 4 (over z), col: 2 (over x), rep: 2 (over core).
Axes of the slice: x: 2, y: 2, z: 4, core: 2. Of those that a mesh axis runs over, the one named last changes fastest.
Arguments:
- tokens: float32 [8192, 512], P(('scene', 'tok'), ('col', 'rep')), parts along dimension 0
- w_qkv: float32 [2, 3, 512, 512], P(None, None, None, ('col', 'rep'))
- w_out: float32 [2, 512, 512], P(None, ('col', 'rep')), may hold values from -0.25 to 0.25
- w_up: float32 [2, 512, 2048], P(None, None, ('col', 'rep')), may hold values from -0.25 to 0.25
- w_down: float32 [2, 2048, 512], P(None, ('col', 'rep')), may hold values from -0.125 to 0.125
- attn_gain: float32 [2, 512], replicated, may hold values from 0.1 to 1.9
- mlp_gain: float32 [2, 512], replicated, may hold values from 0.1 to 1.9
- dest_device: int32 [128], P(('scene', 'tok')), parts along dimension 0, may hold values from 0 to 3, as said below
- dest_slot: int32 [128], P(('scene', 'tok')), parts along dimension 0, may hold values from 0 to 15, as said below
- pillar: int32 [8192], P(('scene', 'tok')), parts along dimension 0, may hold values from -1 to 2047, as said below
- depth_weight: float32 [2, 3, 3, 512], replicated, may hold values from -2 to 2
- point_weight: float32 [2, 512, 1024], replicated, may hold values from -0.25 to 0.25
- raster_gain: float32 [2, 512], replicated, may hold values from 0.1 to 1.9
Outputs:
- raster: float32 [128, 32, 512], P(('scene', 'tok', 'rep'), 'col'), parts along dimension 0
There are 2 independent parts, one for each index of `scene`. A program takes and returns all parts, laid end to end along the dimension named above; an argument that names none is the same for every part. Nothing has to cross between parts.
Inputs may be any that keep to these rules, and one draw needn't show every extreme that they name: `dest_device`: together with dest_slot the blocks fill every index of tok's 16 slots exactly once. At most 5 blocks of one index of tok go to one index, and every index sends exactly 5 blocks to some index. `dest_slot`: the slot of the block among the 16 of its destination. The token at Hilbert position t has a cell in raster rows i * 16 to (i + 1) * 16 - 1 with i = t // 1024, or -1 if it has no pillar; several tokens may share a cell.
All inputs are finite; a program needn't handle non-finite values.
Results may differ from a plain program's by a relative error of at most 0.00012.
Values sent between devices are 32-bit elements; how exact they have to be, the bound alone decides.
A program may use at most 128 MiB of HBM per device.

v0:
```python
import jax
import jax.numpy as jnp
from jax import lax
from jax.sharding import PartitionSpec as P

PATCH = 1024
TR = 16
TC = 16
HD = 16
MATMUL_PRECISION = lax.Precision.HIGHEST
EPSILON = 1e-05


def padded(block, sides, width):
    for axis, dim in sides:
        count = lax.axis_size(axis)
        forward = [(i, i + 1) for i in range(count - 1)]
        backward = [(target, source) for source, target in forward]
        low = lax.ppermute(
            lax.slice_in_dim(block, block.shape[dim] - width, None, axis=dim), axis, forward
        )
        high = lax.ppermute(lax.slice_in_dim(block, 0, width, axis=dim), axis, backward)
        block = jnp.concatenate([low, block, high], axis=dim)
    return block


def layer_norm(values, gain_row):
    average = jnp.mean(values, axis=-1, keepdims=True)
    centered = values - average
    variance = jnp.mean(centered * centered, axis=-1, keepdims=True)
    return centered * lax.rsqrt(variance + EPSILON) * gain_row


def patch_attention(query_projection, key_proj, value_proj):
    scores = jnp.einsum(
        "qhd,khd->hqk", query_projection, key_proj, precision=MATMUL_PRECISION
    ) * HD ** (-0.5)
    scores = scores - jnp.max(scores, axis=-1, keepdims=True)
    weights = jnp.exp(scores)
    weights = weights / jnp.sum(weights, axis=-1, keepdims=True)
    return jnp.einsum("hqk,khd->qhd", weights, value_proj, precision=MATMUL_PRECISION)


def matmul(left, right):
    return jnp.dot(left, right, precision=MATMUL_PRECISION, preferred_element_type=jnp.float32)


def widen(slice_cols):
    return lax.all_gather(slice_cols, ("col", "rep"), axis=1, tiled=True)


def block_layer(stream, layer_index, w_qkv, w_out, w_up, w_down, attn_gain, mlp_gain):
    row_count = stream.shape[0]
    local_cols = w_qkv.shape[-1]
    heads_here = local_cols // HD
    normed = layer_norm(stream, attn_gain[layer_index])
    shaped = tuple(
        (
            matmul(normed, w_qkv[layer_index, j]).reshape(row_count // PATCH, PATCH, heads_here, HD)
            for j in range(3)
        )
    )

    def attend_patch(operands):
        return patch_attention(operands[0], operands[1], operands[2]).reshape(PATCH, local_cols)

    attended = lax.map(attend_patch, shaped).reshape(row_count, local_cols)
    partial_out = matmul(attended, w_out[layer_index])
    stream = stream + lax.psum(partial_out, ("col", "rep"))
    normed = layer_norm(stream, mlp_gain[layer_index])
    hidden = jax.nn.gelu(matmul(normed, w_up[layer_index]), approximate=False)
    partial_mlp = matmul(hidden, w_down[layer_index])
    summed_share = lax.psum_scatter(partial_mlp, ("col", "rep"), scatter_dimension=1, tiled=True)
    feature_width = summed_share.shape[1]
    own_cols = lax.dynamic_slice_in_dim(
        stream, lax.axis_index(("col", "rep")) * feature_width, feature_width, 1
    )
    return own_cols + summed_share


def send_blocks(block_list, dest_device, dest_slot):
    block_count, rows_per_block, feature_width = block_list.shape
    peers = lax.axis_size("tok")
    capacity = max(2, (block_count + peers - 4) // (peers - 1))
    order_index = jnp.arange(block_count, dtype=jnp.int32)
    earlier = (dest_device[:, None] == dest_device[None, :]) & (
        order_index[None, :] < order_index[:, None]
    )
    prior_count = jnp.sum(earlier.astype(jnp.int32), axis=1)
    slot_key = dest_device * capacity + prior_count
    select_entries = (
        jnp.arange(peers * capacity, dtype=jnp.int32)[:, None] == slot_key[None, :]
    ).astype(jnp.float32)
    outgoing = jnp.einsum(
        "jb,brf->jrf", select_entries, block_list, precision=MATMUL_PRECISION
    ).reshape(peers, capacity, rows_per_block, feature_width)
    slot_codes = matmul(select_entries, (dest_slot + 1).astype(jnp.float32)).reshape(
        peers, capacity
    )
    incoming, arrived = (
        lax.all_to_all(outgoing, "tok", split_axis=0, concat_axis=0, tiled=True),
        lax.all_to_all(slot_codes, "tok", split_axis=0, concat_axis=0, tiled=True),
    )
    wanted = (order_index + 1).astype(jnp.float32)
    placing = (wanted[:, None] == arrived.reshape(-1)[None, :]).astype(jnp.float32)
    flat_incoming = incoming.reshape(peers * capacity, rows_per_block, feature_width)
    return jnp.einsum("sj,jrf->srf", placing, flat_incoming, precision=MATMUL_PRECISION)


def raster_cells(extended, depth_weight, point_weight, gain_row):
    row_count = extended.shape[0] - 2
    col_count = extended.shape[1] - 2
    count_of_channels = extended.shape[2]
    normed = (
        extended
        * lax.rsqrt(jnp.mean(extended * extended, axis=-1, keepdims=True) + EPSILON)
        * gain_row
    )
    mixed_cells = jnp.zeros((row_count, col_count, count_of_channels), jnp.float32)
    for row_tap in range(3):
        for col_tap in range(3):
            mixed_cells = (
                mixed_cells
                + normed[row_tap : row_tap + row_count, col_tap : col_tap + col_count]
                * depth_weight[row_tap, col_tap]
            )
    combined = matmul(mixed_cells.reshape(row_count * col_count, count_of_channels), point_weight)
    combined = combined.reshape(row_count, col_count, 2 * count_of_channels)
    centre = extended[1:-1, 1:-1]
    return centre + combined[..., :count_of_channels] * jax.nn.sigmoid(
        combined[..., count_of_channels:]
    )


def on_device(
    tokens,
    w_qkv,
    w_out,
    w_up,
    w_down,
    attn_gain,
    mlp_gain,
    dest_device,
    dest_slot,
    pillar,
    depth_weight,
    point_weight,
    raster_gain,
):
    stream = widen(tokens)
    first_out = block_layer(stream, 0, w_qkv, w_out, w_up, w_down, attn_gain, mlp_gain)
    feature_width = first_out.shape[1]
    block_count = dest_device.shape[0]
    block_list = first_out.reshape(block_count, first_out.shape[0] // block_count, feature_width)
    reordered_tokens = send_blocks(block_list, dest_device, dest_slot)
    stream = widen(reordered_tokens.reshape(-1, feature_width))
    stream = widen(block_layer(stream, 1, w_qkv, w_out, w_up, w_down, attn_gain, mlp_gain))
    rep_rows = TR // lax.axis_size("rep")
    row_start = lax.axis_index(("tok", "rep")) * rep_rows
    col_start = lax.axis_index("col") * TC
    full_width = TC * lax.axis_size("col")
    cell_rows = row_start + jnp.arange(rep_rows, dtype=jnp.int32)[:, None]
    cell_ids = (
        cell_rows * full_width + col_start + jnp.arange(TC, dtype=jnp.int32)[None, :]
    ).reshape(-1)
    onehot = (pillar[:, None] == cell_ids[None, :]).astype(jnp.float32)
    raster = jnp.einsum("tc,td->cd", onehot, stream, precision=MATMUL_PRECISION).reshape(
        rep_rows, TC, -1
    )
    for layer_index in range(2):
        extended = padded(raster, ((("tok", "rep"), 0), ("col", 1)), 1)
        raster = raster_cells(
            extended, depth_weight[layer_index], point_weight[layer_index], raster_gain[layer_index]
        )
    return raster


def solution(mesh):
    placed = (
        P(("scene", "tok"), ("col", "rep")),
        P(None, None, None, ("col", "rep")),
        P(None, ("col", "rep"), None),
        P(None, None, ("col", "rep")),
        P(None, ("col", "rep"), None),
        P(),
        P(),
        P(("scene", "tok")),
        P(("scene", "tok")),
        P(("scene", "tok")),
        P(),
        P(),
        P(),
    )
    return jax.shard_map(
        on_device,
        mesh=mesh,
        in_specs=placed,
        out_specs=P(("scene", "tok", "rep"), "col", None),
        check_vma=False,
    )
```

profile of v0, /device:TPU:1, one launch (start us, length us, event | category | flops | bytes accessed | tf_op | source)
XLA Modules:
  0.0 510.4 jit_solution(3229951573968464027)
XLA Ops:
  9.9 24.3 %all-gather.4.cloned.1.call-done = f32[1024,512]{1,0:T(8,128)} async-done(((f32[1024,128]{1,0:T(8,128)}), f32[1024,512]{1,0:T(8,128)}) %all-gather.4.cloned.1.call-update) | async-done | bytes 2097168 | tf_op jit(solution)/shard_map/all_gather | solution.py:49
  42.0 28.0 %multiply_reduce_fusion.1 = (f32[8,1024]{1,0:T(8,128)S(1)}, f32[8,1024,1024]{1,2,0:T(8,128)S(1)}) fusion(f32[1024,8,16]{0,2,1:T(8,128)S(1)} %fusion.32, f32[1024,8,16]{0,2,1:T(8,128)S(1)} %fusion.30), kind=kOutput, calls=%fused_computation.7 | convolution fusion | flops 1627381760 | bytes 34635776 | tf_op jit(solution)/shard_map/while/body/eval_jaxpr/qhd,khd->hqk/dot_general | solution.py:35
  70.0 5.9 %fusion.4 = f32[8,1024]{1,0:T(8,128)S(1)} fusion(f32[8,1024,1024]{1,2,0:T(8,128)S(1)} %get-tuple-element.80, f32[8,1024]{1,0:T(8,128)S(1)} %get-tuple-element.79), kind=kLoop, calls=%fused_computation.8 | loop fusion | flops 25157632 | bytes 33619968 | tf_op jit(solution)/shard_map/while/body/eval_jaxpr/reduce_sum | solution.py:40
  75.9 5.2 %copy-done = f32[8,1024,1024]{1,2,0:T(8,128)} copy-done((f32[8,1024,1024]{1,2,0:T(8,128)}, f32[8,1024,1024]{1,2,0:T(8,128)S(1)}, u32[]{:S(2)}) %copy-start) | copy-done | bytes 33554456
  81.1 3.4 fusion.34
  84.4 25.6 %fusion.2 = f32[8,16,1024]{2,1,0:T(8,128)S(1)} fusion(f32[1024,8,16]{0,2,1:T(8,128)} %fusion.34, f32[8,1024,1024]{1,2,0:T(8,128)} %copy-done, f32[8,1024]{1,0:T(8,128)S(1)} %fusion.4, f32[8,1024]{1,0:T(8,128)S(1)} %get-tuple-element.79), kind=kOutput, calls=%fused_computation.4 | convolution fusion | flops 1635778560 | bytes 34668544 | tf_op jit(solution)/shard_map/while/body/eval_jaxpr/hqk,khd->qhd/dot_general | solution.py:41
  110.0 4.1 fusion.299
  114.3 50.8 %all-reduce.3.cloned.1.call-done = f32[1024,512]{1,0:T(8,128)} async-done(((f32[1024,512]{1,0:T(8,128)}), f32[1024,512]{1,0:T(8,128)}) %all-reduce.3.cloned.1.call-update) | async-done | bytes 2097168 | tf_op jit(solution)/shard_map/psum | solution.py:69
  169.3 3.7 fusion.143
  173.0 9.5 %fusion.14 = f32[1024,512]{1,0:T(8,128)} fusion(f32[1024,512]{1,0:T(8,128)S(1)} %fusion.143, f32[2,512,512]{2,1,0:T(8,128)S(1)} %copy-done.15), kind=kOutput, calls=%fused_computation.20 | convolution fusion | flops 3254779904 | bytes 5242880 | tf_op jit(solution)/shard_map/dot_general | solution.py:45
  184.1 4.3 all-to-all-start
  188.5 25.5 %reduce-scatter.3.cloned.1.call-done = f32[1024,128]{1,0:T(8,128)} async-done(((f32[1024,512]{1,0:T(8,128)}), f32[1024,128]{1,0:T(8,128)}) %reduce-scatter.3.cloned.1.call-update) | async-done | bytes 524304 | tf_op jit(solution)/shard_map/reduce_scatter | solution.py:73
  217.1 4.3 all-to-all-start.1
  222.7 15.6 %all-to-all-done.1 = f32[4,5,64,128]{3,2,1,0:T(8,128)S(1)} async-done(((f32[4,5,64,128]{3,2,1,0:T(8,128)}), f32[4,5,64,128]{3,2,1,0:T(8,128)S(1)}, u32[]{:S(2)}, u32[]{:S(2)}) %all-to-all-start.1) | async-done | bytes 655392 | tf_op jit(solution)/shard_map/all_to_all | solution.py:101
  240.6 21.8 %all-gather.6.cloned.1.call-done = f32[1024,512]{1,0:T(8,128)} async-done(((f32[1024,128]{1,0:T(8,128)}), f32[1024,512]{1,0:T(8,128)}) %all-gather.6.cloned.1.call-update) | async-done | bytes 2097168 | tf_op jit(solution)/shard_map/all_gather | solution.py:49
  270.1 27.9 %multiply_reduce_fusion = (f32[8,1024]{1,0:T(8,128)S(1)}, f32[8,1024,1024]{1,2,0:T(8,128)S(1)}) fusion(f32[1024,8,16]{0,2,1:T(8,128)S(1)} %fusion.26, f32[1024,8,16]{0,2,1:T(8,128)S(1)} %fusion.24), kind=kOutput, calls=%fused_computation.6 | convolution fusion | flops 1627381760 | bytes 34635776 | tf_op jit(solution)/shard_map/while/body/eval_jaxpr/qhd,khd->hqk/dot_general | solution.py:35
  298.0 5.9 %fusion.5 = f32[8,1024]{1,0:T(8,128)S(1)} fusion(f32[8,1024,1024]{1,2,0:T(8,128)S(1)} %get-tuple-element.82, f32[8,1024]{1,0:T(8,128)S(1)} %get-tuple-element.81), kind=kLoop, calls=%fused_computation.9 | loop fusion | flops 25157632 | bytes 33619968 | tf_op jit(solution)/shard_map/while/body/eval_jaxpr/reduce_sum | solution.py:40
  303.9 5.2 %copy-done.1 = f32[8,1024,1024]{1,2,0:T(8,128)} copy-done((f32[8,1024,1024]{1,2,0:T(8,128)}, f32[8,1024,1024]{1,2,0:T(8,128)S(1)}, u32[]{:S(2)}) %copy-start.1) | copy-done | bytes 33554456
  311.7 25.0 %fusion = f32[8,16,1024]{2,1,0:T(8,128)S(1)} fusion(f32[1024,8,16]{0,2,1:T(8,128)S(1)} %fusion.28, f32[8,1024,1024]{1,2,0:T(8,128)} %copy-done.1, f32[8,1024]{1,0:T(8,128)S(1)} %fusion.5, f32[8,1024]{1,0:T(8,128)S(1)} %get-tuple-element.81), kind=kOutput, calls=%fused_computation.2 | convolution fusion | flops 1635778560 | bytes 34668544 | tf_op jit(solution)/shard_map/while/body/eval_jaxpr/hqk,khd->qhd/dot_general | solution.py:41
  336.7 4.1 fusion.297
  340.8 50.8 %all-reduce.5.cloned.1.call-done = f32[1024,512]{1,0:T(8,128)} async-done(((f32[1024,512]{1,0:T(8,128)}), f32[1024,512]{1,0:T(8,128)}) %all-reduce.5.cloned.1.call-update) | async-done | bytes 2097168 | tf_op jit(solution)/shard_map/psum | solution.py:69
  395.9 3.7 fusion.89
  399.6 9.5 %fusion.18 = f32[1024,512]{1,0:T(8,128)} fusion(f32[1024,512]{1,0:T(8,128)S(1)} %fusion.89, f32[2,512,512]{2,1,0:T(8,128)S(1)} %copy-done.16), kind=kOutput, calls=%fused_computation.23 | convolution fusion | flops 3254779904 | bytes 5242880 | tf_op jit(solution)/shard_map/dot_general | solution.py:45
  409.2 31.4 %reduce-scatter.5.cloned.1.call-done = f32[1024,128]{1,0:T(8,128)} async-done(((f32[1024,512]{1,0:T(8,128)}), f32[1024,128]{1,0:T(8,128)}) %reduce-scatter.5.cloned.1.call-update) | async-done | bytes 524304 | tf_op jit(solution)/shard_map/reduce_scatter | solution.py:73
  442.9 23.3 %all-gather.8.cloned.1.call-done = f32[1024,512]{1,0:T(8,128)} async-done(((f32[1024,128]{1,0:T(8,128)}), f32[1024,512]{1,0:T(8,128)}) %all-gather.8.cloned.1.call-update) | async-done | bytes 2097168 | tf_op jit(solution)/shard_map/all_gather | solution.py:49
  466.3 2.8 fusion.253
  469.1 3.3 collective-permute-start
  474.3 3.3 collective-permute-done.1
  481.1 3.2 collective-permute-done.3
  486.2 3.3 collective-permute-start.4
  491.5 3.3 collective-permute-done.5
  497.6 3.2 collective-permute-done.7
  (128 shorter events, 55.0 us)
Async XLA Ops:
  6.5 27.7 %all-gather.4.cloned.1.call-start = ((), (), s32[]{:S(2)}) async-start(), calls=%async_computation.4 | async-start | bytes 2621440 | tf_op jit(solution)/shard_map/all_gather | solution.py:49
  7.3 2.6 copy-start.10
  7.3 157.8 %all-reduce.3.cloned.1.call-start = ((), (), s32[]{:S(2)}) async-start(), calls=%async_computation.5 | async-start | bytes 4194304 | tf_op jit(solution)/shard_map/psum | solution.py:69
  36.4 3.0 copy-start.8
  70.0 11.1 %copy-start = (f32[8,1024,1024]{1,2,0:T(8,128)}, f32[8,1024,1024]{1,2,0:T(8,128)S(1)}, u32[]{:S(2)}) copy-start(f32[8,1024,1024]{1,2,0:T(8,128)S(1)} %get-tuple-element.80) | copy-start | bytes 100663296
  110.0 4.2 copy-start.11
  114.2 99.8 %reduce-scatter.3.cloned.1.call-start = ((), (), s32[]{:S(2)}) async-start(), calls=%async_computation.6 | async-start | bytes 2621440 | tf_op jit(solution)/shard_map/reduce_scatter | solution.py:73
  166.9 6.0 %copy-start.4 = (f32[1024,512]{1,0:T(8,128)}, f32[1024,512]{1,0:T(8,128)S(1)}, u32[]{:S(2)}) copy-start(f32[1024,512]{1,0:T(8,128)S(1)} %get-tuple-element.31) | copy-start | bytes 6291460
  167.0 2.4 copy-start.6
  169.3 3.7 copy-start.15
  184.1 33.0 %all-to-all-start = ((f32[4,1,5]{2,1,0:T(1,128)}), f32[4,1,5]{2,1,0:T(1,128)S(1)}, u32[]{:S(2)}, u32[]{:S(2)}) async-start(f32[4,1,5]{2,1,0:T(1,128)} %bitcast.2), calls=%async_computation | async-start | bytes 4096 | tf_op jit(solution)/shard_map/all_to_all | solution.py:102
  217.1 21.2 %all-to-all-start.1 = ((f32[4,5,64,128]{3,2,1,0:T(8,128)}), f32[4,5,64,128]{3,2,1,0:T(8,128)S(1)}, u32[]{:S(2)}, u32[]{:S(2)}) async-start(f32[4,5,64,128]{3,2,1,0:T(8,128)} %copy.48), calls=%async_computation.2 | async-start | bytes 1310720 | tf_op jit(solution)/shard_map/all_to_all | solution.py:101
  221.5 40.9 %all-gather.6.cloned.1.call-start = ((), (), s32[]{:S(2)}) async-start(), calls=%async_computation.7 | async-start | bytes 2621440 | tf_op jit(solution)/shard_map/all_gather | solution.py:49
  240.1 151.6 %all-reduce.5.cloned.1.call-start = ((), (), s32[]{:S(2)}) async-start(), calls=%async_computation.8 | async-start | bytes 4194304 | tf_op jit(solution)/shard_map/psum | solution.py:69
  298.0 11.1 %copy-start.1 = (f32[8,1024,1024]{1,2,0:T(8,128)}, f32[8,1024,1024]{1,2,0:T(8,128)S(1)}, u32[]{:S(2)}) copy-start(f32[8,1024,1024]{1,2,0:T(8,128)S(1)} %get-tuple-element.82) | copy-start | bytes 100663296
  340.8 99.8 %reduce-scatter.5.cloned.1.call-start = ((), (), s32[]{:S(2)}) async-start(), calls=%async_computation.9 | async-start | bytes 2621440 | tf_op jit(solution)/shard_map/reduce_scatter | solution.py:73
  393.6 6.0 %copy-start.5 = (f32[1024,512]{1,0:T(8,128)}, f32[1024,512]{1,0:T(8,128)S(1)}, u32[]{:S(2)}) copy-start(f32[1024,512]{1,0:T(8,128)S(1)} %get-tuple-element.24) | copy-start | bytes 6291460
  393.6 2.4 copy-start.7
  395.9 3.7 copy-start.16
  409.1 33.7 %copy-start.9 = (f32[2,3,3,512]{3,0,2,1:T(2,128)S(1)}, f32[2,3,3,512]{3,0,2,1:T(2,128)}, u32[]{:S(2)}) copy-start(f32[2,3,3,512]{3,0,2,1:T(2,128)} %param.23) | copy-start | bytes 110596
  409.1 57.1 %copy-start.13 = (s32[1024]{0:T(1024)S(1)}, s32[1024]{0:T(1024)}, u32[]{:S(2)}) copy-start(s32[1024]{0:T(1024)} %param.22) | copy-start | bytes 12292
  409.1 57.1 %all-gather.8.cloned.1.call-start = ((), (), s32[]{:S(2)}) async-start(), calls=%async_computation.10 | async-start | bytes 2621440 | tf_op jit(solution)/shard_map/all_gather | solution.py:49
  442.7 38.5 %copy-start.12 = (f32[2,512]{1,0:T(2,128)S(1)}, f32[2,512]{1,0:T(2,128)}, u32[]{:S(2)}) copy-start(f32[2,512]{1,0:T(2,128)} %param.25) | copy-start | bytes 12292
  466.3 18.4 %copy-start.14 = (f32[2,512,1024]{2,1,0:T(8,128)S(1)}, f32[2,512,1024]{2,1,0:T(8,128)}, u32[]{:S(2)}) copy-start(f32[2,512,1024]{2,1,0:T(8,128)} %param.24) | copy-start | bytes 12582916
  469.1 5.2 %collective-permute-start = (f32[1,16,512]{2,1,0:T(8,128)S(1)}, f32[1,16,512]{2,1,0:T(8,128)S(1)}, u32[]{:S(2)}, u32[]{:S(2)}) collective-permute-start(f32[1,16,512]{2,1,0:T(8,128)S(1)} %get-tuple-element.51), channel_id=1, source_target_pairs={{0,1},{1,4},{4,5},{5,8},{8,9},{9,12},{12,13},{2,3},{3,6},{6,7},{7,... | collective-permute-start | bytes 98312 | tf_op jit(solution)/shard_map/ppermute | solution.py:19
  472.4 5.2 %collective-permute-start.1 = (f32[1,16,512]{2,1,0:T(8,128)S(1)}, f32[1,16,512]{2,1,0:T(8,128)S(1)}, u32[]{:S(2)}, u32[]{:S(2)}) collective-permute-start(f32[1,16,512]{2,1,0:T(8,128)S(1)} %get-tuple-element.52), channel_id=1, source_target_pairs={{1,0},{4,1},{5,4},{8,5},{9,8},{12,9},{13,12},{3,2},{6,3},{7,6},{10... | collective-permute-start | bytes 98312 | tf_op jit(solution)/shard_map/ppermute | solution.py:22
  477.6 3.5 collective-permute-start.2
  479.8 4.5 collective-permute-start.3
  486.2 5.3 %collective-permute-start.4 = (f32[1,16,512]{2,1,0:T(8,128)S(1)}, f32[1,16,512]{2,1,0:T(8,128)S(1)}, u32[]{:S(2)}, u32[]{:S(2)}) collective-permute-start(f32[1,16,512]{2,1,0:T(8,128)S(1)} %get-tuple-element.49), channel_id=1, source_target_pairs={{0,1},{1,4},{4,5},{5,8},{8,9},{9,12},{12,13},{2,3},{3,6},{6,7},{7,... | collective-permute-start | bytes 98312 | tf_op jit(solution)/shard_map/ppermute | solution.py:19
  489.6 5.2 %collective-permute-start.5 = (f32[1,16,512]{2,1,0:T(8,128)S(1)}, f32[1,16,512]{2,1,0:T(8,128)S(1)}, u32[]{:S(2)}, u32[]{:S(2)}) collective-permute-start(f32[1,16,512]{2,1,0:T(8,128)S(1)} %get-tuple-element.50), channel_id=1, source_target_pairs={{1,0},{4,1},{5,4},{8,5},{9,8},{12,9},{13,12},{3,2},{6,3},{7,6},{10... | collective-permute-start | bytes 98312 | tf_op jit(solution)/shard_map/ppermute | solution.py:22
  494.9 2.7 collective-permute-start.6
  496.2 4.5 collective-permute-start.7
  (4 other events, 5.9 us)
Sparse Core Ops, SparseCore 0:
  8.9 25.2 all-gather.3
  114.3 50.7 all-reduce.2
  182.6 31.3 reduce-scatter.2
  240.2 22.0 all-gather.5
  340.9 50.7 all-reduce.4
  409.3 31.2 reduce-scatter.4
  442.8 23.4 all-gather.7
where the time goes:
time: 515 us; the launch traced here: 510 us
  waiting for transfers between devices  257 us (50%)
  matrix products  165 us (32%)
  other arithmetic  27 us (5%)
  starting transfers between devices  25.4 us (5%)
  local copies, waits for them, and re-layouts  21.6 us (4%)
  between operations  14.3 us (3%)
    psum x2, waiting for transfers between devices, block_layer(): stream = stream + lax.psum(partial_out, ('col', 'rep'))  102 us
    all_gather x3, waiting for transfers between devices, widen(): return lax.all_gather(slice_cols, ('col', 'rep'), axis=1, tiled=True)  69.4 us
    reduce_scatter x2, waiting for transfers between devices, block_layer(): lax.psum_scatter(partial_mlp, ('col', 'rep'), scatter_dimension=1, tiled=...  56.9 us
    dot_general x2, matrix products, patch_attention(): jnp.einsum('qhd,khd->hqk', query_projection, key_proj, precision=MATMUL_P...  56 us
    dot_general x15, matrix products, matmul(): jnp.dot(left, right, precision=MATMUL_PRECISION, preferred_element_type=j...  53.7 us
    dot_general x2, matrix products, patch_attention(): jnp.einsum('hqk,khd->qhd', weights, value_proj, precision=MATMUL_PRECISION)  50.6 us
    unnamed x45, local copies, waits for them, and re-layouts  16.8 us
    all_to_all x1, waiting for transfers between devices, send_blocks(): lax.all_to_all(outgoing, 'tok', split_axis=0, concat_axis=0, tiled=True)  15.6 us
  transfers between devices with their start and end apart: 17, of which 12 were waited for; matrix products, arithmetic and copies ran while one was open for 2% of the time, Pallas kernels for 0%

commit v1 on v0

--- a/solution.py
+++ b/solution.py
@@ -66,7 +66,7 @@
 
     attended = lax.map(attend_patch, shaped).reshape(row_count, local_cols)
     partial_out = matmul(attended, w_out[layer_index])
-    stream = stream + lax.psum(partial_out, ("col", "rep"))
+    stream = stream + jnp.sum(lax.all_gather(partial_out, ("col", "rep")), axis=0)
     normed = layer_norm(stream, mlp_gain[layer_index])
     hidden = jax.nn.gelu(matmul(normed, w_up[layer_index]), approximate=False)
     partial_mlp = matmul(hidden, w_down[layer_index])

time: 515 us -> 541 us (1.050)
  waiting for transfers between devices: 257 us -> 270 us
  other arithmetic: 27 us -> 39 us
    all_gather x0 -> x2, waiting for transfers between devices: none -> 116 us  [block_layer(): lax.all_gather(partial_out, ('col', 'rep'))]
    psum x2 -> x0, waiting for transfers between devices: 102 us -> none  [block_layer(): stream = stream + lax.psum(partial_out, ('col', 'rep'))]
    reduce_sum x0 -> x2, other arithmetic: none -> 12 us  [block_layer(): jnp.sum(lax.all_gather(partial_out, ('col', 'rep')), axis=0)]
  transfers between devices with their start and end apart: 17 -> 17, of which waited for: 12 -> 12; matrix products, arithmetic and copies ran while one was open for 2% -> 1% of each run, Pallas kernels for 0% -> 0%
where the time goes in v1:
time: 541 us; the launch traced here: 536 us
  waiting for transfers between devices  270 us (50%)
  matrix products  164 us (30%)
  other arithmetic  39 us (7%)
  starting transfers between devices  26.2 us (5%)
  local copies, waits for them, and re-layouts  21.6 us (4%)
  between operations  14.3 us (3%)
    all_gather x2, waiting for transfers between devices, block_layer(): lax.all_gather(partial_out, ('col', 'rep'))  116 us
    all_gather x3, waiting for transfers between devices, widen(): return lax.all_gather(slice_cols, ('col', 'rep'), axis=1, tiled=True)  69.2 us
    dot_general x2, matrix products, patch_attention(): jnp.einsum('qhd,khd->hqk', query_projection, key_proj, precision=MATMUL_P...  55.7 us
    reduce_scatter x2, waiting for transfers between devices, block_layer(): lax.psum_scatter(partial_mlp, ('col', 'rep'), scatter_dimension=1, tiled=...  55.4 us
    dot_general x15, matrix products, matmul(): jnp.dot(left, right, precision=MATMUL_PRECISION, preferred_element_type=j...  53.5 us
    dot_general x2, matrix products, patch_attention(): jnp.einsum('hqk,khd->qhd', weights, value_proj, precision=MATMUL_PRECISION)  50.6 us
    unnamed x45, local copies, waits for them, and re-layouts  16.8 us
    all_to_all x1, waiting for transfers between devices, send_blocks(): lax.all_to_all(outgoing, 'tok', split_axis=0, concat_axis=0, tiled=True)  15.6 us
  transfers between devices with their start and end apart: 17, of which 12 were waited for; matrix products, arithmetic and copies ran while one was open for 1% of the time, Pallas kernels for 0%

profile of v1, /device:TPU:1, one launch (start us, length us, event | category | flops | bytes accessed | tf_op | source)
XLA Modules:
  0.0 535.6 jit_solution(18016972037036801910)
XLA Ops:
  9.9 24.3 %all-gather.8.cloned.1.call-done = f32[1024,512]{1,0:T(8,128)} async-done(((f32[1024,128]{1,0:T(8,128)}), f32[1024,512]{1,0:T(8,128)}) %all-gather.8.cloned.1.call-update) | async-done | bytes 2097168 | tf_op jit(solution)/shard_map/all_gather | solution.py:49
  42.0 28.0 %multiply_reduce_fusion.1 = (f32[8,1024]{1,0:T(8,128)S(1)}, f32[8,1024,1024]{1,2,0:T(8,128)S(1)}) fusion(f32[1024,8,16]{0,2,1:T(8,128)S(1)} %fusion.32, f32[1024,8,16]{0,2,1:T(8,128)S(1)} %fusion.30), kind=kOutput, calls=%fused_computation.7 | convolution fusion | flops 1627381760 | bytes 34635776 | tf_op jit(solution)/shard_map/while/body/eval_jaxpr/qhd,khd->hqk/dot_general | solution.py:35
  70.0 5.9 %fusion.4 = f32[8,1024]{1,0:T(8,128)S(1)} fusion(f32[8,1024,1024]{1,2,0:T(8,128)S(1)} %get-tuple-element.80, f32[8,1024]{1,0:T(8,128)S(1)} %get-tuple-element.79), kind=kLoop, calls=%fused_computation.8 | loop fusion | flops 25157632 | bytes 33619968 | tf_op jit(solution)/shard_map/while/body/eval_jaxpr/reduce_sum | solution.py:40
  75.9 5.2 copy-done
  81.1 3.4 fusion.34
  84.4 25.6 %fusion.2 = f32[8,16,1024]{2,1,0:T(8,128)S(1)} fusion(f32[1024,8,16]{0,2,1:T(8,128)} %fusion.34, f32[8,1024,1024]{1,2,0:T(8,128)} %copy-done, f32[8,1024]{1,0:T(8,128)S(1)} %fusion.4, f32[8,1024]{1,0:T(8,128)S(1)} %get-tuple-element.79), kind=kOutput, calls=%fused_computation.4 | convolution fusion | flops 1635778560 | bytes 34668544 | tf_op jit(solution)/shard_map/while/body/eval_jaxpr/hqk,khd->qhd/dot_general | solution.py:41
  110.0 4.2 fusion.299
  114.5 58.2 %all-gather.14.cloned.1.call-done = f32[4096,512]{1,0:T(8,128)} async-done(((f32[1024,512]{1,0:T(8,128)}), f32[4096,512]{1,0:T(8,128)}) %all-gather.14.cloned.1.call-update) | async-done | bytes 8388624 | tf_op jit(solution)/shard_map/all_gather | solution.py:69
  172.7 6.0 %reduce_sum.141 = f32[1024,512]{1,0:T(8,128)} reduce(f32[4,1024,512]{2,1,0:T(8,128)} %bitcast.152, f32[]{:T(128)} %constant.35.clone.1), dimensions={0}, to_apply=%region_5.6 | reduce | flops 1572864 | bytes 10485764 | tf_op jit(solution)/shard_map/reduce_sum | solution.py:69
  182.9 3.7 fusion.143
  186.6 9.3 %fusion.14 = f32[1024,512]{1,0:T(8,128)} fusion(f32[1024,512]{1,0:T(8,128)S(1)} %fusion.143, f32[2,512,512]{2,1,0:T(8,128)S(1)} %copy-done.15), kind=kOutput, calls=%fused_computation.20 | convolution fusion | flops 3254779904 | bytes 5242880 | tf_op jit(solution)/shard_map/dot_general | solution.py:45
  197.6 4.3 all-to-all-start
  201.9 24.8 %reduce-scatter.3.cloned.1.call-done = f32[1024,128]{1,0:T(8,128)} async-done(((f32[1024,512]{1,0:T(8,128)}), f32[1024,128]{1,0:T(8,128)}) %reduce-scatter.3.cloned.1.call-update) | async-done | bytes 524304 | tf_op jit(solution)/shard_map/reduce_scatter | solution.py:73
  229.8 4.3 all-to-all-start.1
  235.4 15.6 %all-to-all-done.1 = f32[4,5,64,128]{3,2,1,0:T(8,128)S(1)} async-done(((f32[4,5,64,128]{3,2,1,0:T(8,128)}), f32[4,5,64,128]{3,2,1,0:T(8,128)S(1)}, u32[]{:S(2)}, u32[]{:S(2)}) %all-to-all-start.1) | async-done | bytes 655392 | tf_op jit(solution)/shard_map/all_to_all | solution.py:101
  253.4 21.6 %all-gather.10.cloned.1.call-done = f32[1024,512]{1,0:T(8,128)} async-done(((f32[1024,128]{1,0:T(8,128)}), f32[1024,512]{1,0:T(8,128)}) %all-gather.10.cloned.1.call-update) | async-done | bytes 2097168 | tf_op jit(solution)/shard_map/all_gather | solution.py:49
  282.8 27.7 %multiply_reduce_fusion = (f32[8,1024]{1,0:T(8,128)S(1)}, f32[8,1024,1024]{1,2,0:T(8,128)S(1)}) fusion(f32[1024,8,16]{0,2,1:T(8,128)S(1)} %fusion.26, f32[1024,8,16]{0,2,1:T(8,128)S(1)} %fusion.24), kind=kOutput, calls=%fused_computation.6 | convolution fusion | flops 1627381760 | bytes 34635776 | tf_op jit(solution)/shard_map/while/body/eval_jaxpr/qhd,khd->hqk/dot_general | solution.py:35
  310.5 5.9 %fusion.5 = f32[8,1024]{1,0:T(8,128)S(1)} fusion(f32[8,1024,1024]{1,2,0:T(8,128)S(1)} %get-tuple-element.82, f32[8,1024]{1,0:T(8,128)S(1)} %get-tuple-element.81), kind=kLoop, calls=%fused_computation.9 | loop fusion | flops 25157632 | bytes 33619968 | tf_op jit(solution)/shard_map/while/body/eval_jaxpr/reduce_sum | solution.py:40
  316.4 5.2 copy-done.1
  324.1 25.0 %fusion = f32[8,16,1024]{2,1,0:T(8,128)S(1)} fusion(f32[1024,8,16]{0,2,1:T(8,128)S(1)} %fusion.28, f32[8,1024,1024]{1,2,0:T(8,128)} %copy-done.1, f32[8,1024]{1,0:T(8,128)S(1)} %fusion.5, f32[8,1024]{1,0:T(8,128)S(1)} %get-tuple-element.81), kind=kOutput, calls=%fused_computation.2 | convolution fusion | flops 1635778560 | bytes 34668544 | tf_op jit(solution)/shard_map/while/body/eval_jaxpr/hqk,khd->qhd/dot_general | solution.py:41
  349.1 4.2 fusion.297
  353.5 58.2 %all-gather.16.cloned.1.call-done = f32[4096,512]{1,0:T(8,128)} async-done(((f32[1024,512]{1,0:T(8,128)}), f32[4096,512]{1,0:T(8,128)}) %all-gather.16.cloned.1.call-update) | async-done | bytes 8388624 | tf_op jit(solution)/shard_map/all_gather | solution.py:69
  411.7 6.0 %reduce_sum.147 = f32[1024,512]{1,0:T(8,128)} reduce(f32[4,1024,512]{2,1,0:T(8,128)} %bitcast.153, f32[]{:T(128)} %constant.35.clone.1), dimensions={0}, to_apply=%region_13.14 | reduce | flops 1572864 | bytes 10485764 | tf_op jit(solution)/shard_map/reduce_sum | solution.py:69
  422.0 3.7 fusion.89
  425.6 9.3 %fusion.18 = f32[1024,512]{1,0:T(8,128)} fusion(f32[1024,512]{1,0:T(8,128)S(1)} %fusion.89, f32[2,512,512]{2,1,0:T(8,128)S(1)} %copy-done.16), kind=kOutput, calls=%fused_computation.23 | convolution fusion | flops 3254779904 | bytes 5242880 | tf_op jit(solution)/shard_map/dot_general | solution.py:45
  435.1 30.7 %reduce-scatter.5.cloned.1.call-done = f32[1024,128]{1,0:T(8,128)} async-done(((f32[1024,512]{1,0:T(8,128)}), f32[1024,128]{1,0:T(8,128)}) %reduce-scatter.5.cloned.1.call-update) | async-done | bytes 524304 | tf_op jit(solution)/shard_map/reduce_scatter | solution.py:73
  468.1 23.3 %all-gather.12.cloned.1.call-done = f32[1024,512]{1,0:T(8,128)} async-done(((f32[1024,128]{1,0:T(8,128)}), f32[1024,512]{1,0:T(8,128)}) %all-gather.12.cloned.1.call-update) | async-done | bytes 2097168 | tf_op jit(solution)/shard_map/all_gather | solution.py:49
  494.2 3.3 collective-permute-start
  499.4 3.3 collective-permute-done.1
  511.4 3.3 collective-permute-start.4
  516.7 3.3 collective-permute-done.5
  522.7 3.2 collective-permute-done.7
  (130 shorter events, 61.5 us)
Async XLA Ops:
  6.5 27.7 %all-gather.8.cloned.1.call-start = ((), (), s32[]{:S(2)}) async-start(), calls=%async_computation.4 | async-start | bytes 2621440 | tf_op jit(solution)/shard_map/all_gather | solution.py:49
  7.3 2.6 copy-start.10
  7.3 165.4 %all-gather.14.cloned.1.call-start = ((), (), s32[]{:S(2)}) async-start(), calls=%async_computation.9 | async-start | bytes 10485760 | tf_op jit(solution)/shard_map/all_gather | solution.py:69
  36.4 3.0 copy-start.8
  70.0 11.1 %copy-start = (f32[8,1024,1024]{1,2,0:T(8,128)}, f32[8,1024,1024]{1,2,0:T(8,128)S(1)}, u32[]{:S(2)}) copy-start(f32[8,1024,1024]{1,2,0:T(8,128)S(1)} %get-tuple-element.80) | copy-start | bytes 100663296
  110.0 4.4 copy-start.11
  114.2 112.4 %reduce-scatter.3.cloned.1.call-start = ((), (), s32[]{:S(2)}) async-start(), calls=%async_computation.5 | async-start | bytes 2621440 | tf_op jit(solution)/shard_map/reduce_scatter | solution.py:73
  180.5 6.0 %copy-start.4 = (f32[1024,512]{1,0:T(8,128)}, f32[1024,512]{1,0:T(8,128)S(1)}, u32[]{:S(2)}) copy-start(f32[1024,512]{1,0:T(8,128)S(1)} %get-tuple-element.31) | copy-start | bytes 6291460
  180.6 2.4 copy-start.6
  182.9 3.7 copy-start.15
  197.6 32.2 %all-to-all-start = ((f32[4,1,5]{2,1,0:T(1,128)}), f32[4,1,5]{2,1,0:T(1,128)S(1)}, u32[]{:S(2)}, u32[]{:S(2)}) async-start(f32[4,1,5]{2,1,0:T(1,128)} %bitcast.2), calls=%async_computation | async-start | bytes 4096 | tf_op jit(solution)/shard_map/all_to_all | solution.py:102
  229.8 21.2 %all-to-all-start.1 = ((f32[4,5,64,128]{3,2,1,0:T(8,128)}), f32[4,5,64,128]{3,2,1,0:T(8,128)S(1)}, u32[]{:S(2)}, u32[]{:S(2)}) async-start(f32[4,5,64,128]{3,2,1,0:T(8,128)} %copy.48), calls=%async_computation.2 | async-start | bytes 1310720 | tf_op jit(solution)/shard_map/all_to_all | solution.py:101
  234.1 40.9 %all-gather.10.cloned.1.call-start = ((), (), s32[]{:S(2)}) async-start(), calls=%async_computation.6 | async-start | bytes 2621440 | tf_op jit(solution)/shard_map/all_gather | solution.py:49
  252.8 159.0 %all-gather.16.cloned.1.call-start = ((), (), s32[]{:S(2)}) async-start(), calls=%async_computation.10 | async-start | bytes 10485760 | tf_op jit(solution)/shard_map/all_gather | solution.py:69
  310.5 11.1 %copy-start.1 = (f32[8,1024,1024]{1,2,0:T(8,128)}, f32[8,1024,1024]{1,2,0:T(8,128)S(1)}, u32[]{:S(2)}) copy-start(f32[8,1024,1024]{1,2,0:T(8,128)S(1)} %get-tuple-element.82) | copy-start | bytes 100663296
  353.3 112.4 %reduce-scatter.5.cloned.1.call-start = ((), (), s32[]{:S(2)}) async-start(), calls=%async_computation.7 | async-start | bytes 2621440 | tf_op jit(solution)/shard_map/reduce_scatter | solution.py:73
  419.6 6.0 %copy-start.5 = (f32[1024,512]{1,0:T(8,128)}, f32[1024,512]{1,0:T(8,128)S(1)}, u32[]{:S(2)}) copy-start(f32[1024,512]{1,0:T(8,128)S(1)} %get-tuple-element.24) | copy-start | bytes 6291460
  419.6 2.4 copy-start.7
  422.0 3.7 copy-start.16
  435.0 33.0 %copy-start.9 = (f32[2,3,3,512]{3,0,2,1:T(2,128)S(1)}, f32[2,3,3,512]{3,0,2,1:T(2,128)}, u32[]{:S(2)}) copy-start(f32[2,3,3,512]{3,0,2,1:T(2,128)} %param.23) | copy-start | bytes 110596
  435.0 56.4 %copy-start.13 = (s32[1024]{0:T(1024)S(1)}, s32[1024]{0:T(1024)}, u32[]{:S(2)}) copy-start(s32[1024]{0:T(1024)} %param.22) | copy-start | bytes 12292
  435.0 56.4 %all-gather.12.cloned.1.call-start = ((), (), s32[]{:S(2)}) async-start(), calls=%async_computation.8 | async-start | bytes 2621440 | tf_op jit(solution)/shard_map/all_gather | solution.py:49
  467.8 38.7 %copy-start.12 = (f32[2,512]{1,0:T(2,128)S(1)}, f32[2,512]{1,0:T(2,128)}, u32[]{:S(2)}) copy-start(f32[2,512]{1,0:T(2,128)} %param.25) | copy-start | bytes 12292
  491.4 18.4 %copy-start.14 = (f32[2,512,1024]{2,1,0:T(8,128)S(1)}, f32[2,512,1024]{2,1,0:T(8,128)}, u32[]{:S(2)}) copy-start(f32[2,512,1024]{2,1,0:T(8,128)} %param.24) | copy-start | bytes 12582916
  494.2 5.2 collective-permute-start
  497.5 5.2 collective-permute-start.1
  502.8 3.7 collective-permute-start.2
  504.9 4.5 collective-permute-start.3
  511.4 5.3 collective-permute-start.4
  514.7 5.2 collective-permute-start.5
  520.0 2.7 collective-permute-start.6
  521.4 4.5 collective-permute-start.7
  (4 other events, 5.9 us)
Sparse Core Ops, SparseCore 0:
  8.9 25.2 all-gather.7
  114.4 58.2 all-gather.13
  196.1 30.5 reduce-scatter.2
  252.9 22.0 all-gather.9
  353.4 58.2 all-gather.15
  435.1 30.5 reduce-scatter.4
  467.9 23.3 all-gather.11
